TPU v7x, 32 devices: a whole 2x2x4 slice. The times are simulated.
32 devices in a mesh: dp: 4 (over y, x), mp: 8 (over z, core).
Axes of the slice: x: 2, y: 2, z: 4, core: 2. Of those that a mesh axis runs over, the one named last changes fastest.
Arguments:
- residual_in: bfloat16 [512, 3584], P('dp', 'mp'), may hold values from -6 to 6
- pre_gain: float32 [3584], replicated, may hold values from 0.5 to 1.5
- post_gain: float32 [3584], replicated, may hold values from 0.5 to 1.5
- w_gate: bfloat16 [3584, 14336], P(None, 'mp'), may hold values from -0.09375 to 0.09375
- w_up: bfloat16 [3584, 14336], P(None, 'mp'), may hold values from -0.09375 to 0.09375
- w_down: bfloat16 [14336, 3584], P('mp'), may hold values from -0.046875 to 0.046875
- w_enc: bfloat16 [3584, 16384], P(None, ('dp', 'mp')), may hold values from -0.09375 to 0.09375
- b_enc: float32 [16384], P(('dp', 'mp')), may hold values from -2.5 to 2.5
- threshold: float32 [16384], P(('dp', 'mp')), may hold values from 0.1 to 1
- w_dec: bfloat16 [16384, 3584], P(('dp', 'mp')), may hold values from -0.046875 to 0.046875
- b_dec: float32 [3584], replicated, may hold values from -1.5 to 1.5
Outputs:
- loss_value: float32 [], replicated
- d_w_enc: bfloat16 [3584, 16384], P(None, ('dp', 'mp'))
- d_w_dec: bfloat16 [16384, 3584], P(('dp', 'mp'))
- d_b_enc: float32 [16384], P(('dp', 'mp'))
- d_threshold: float32 [16384], P(('dp', 'mp'))
- d_b_dec: float32 [3584], replicated
All inputs are finite; a program needn't handle non-finite values.
Results may differ from a plain program's by a relative error of at most 0.014.
The roundings to bfloat16 on the way count: a program that leaves them out, or rounds other values in their place, can miss the bound.
Values may be sent and summed in bfloat16 or wider, within the bound.
No kernel may reach another device: no remote copies, remote signals or barrier semaphores. Data moves between devices by JAX's collectives and lax.ppermute only.
A program may use at most 128 MiB of HBM per device.

v0:
```python
import jax
import jax.numpy as jnp
from jax import lax
from jax.sharding import PartitionSpec as P

norm_eps = 1e-06
gate_band = 0.1
sparsity_coef = 0.05


def contract_first(left, right):
    return lax.dot_general(
        left, right, (((0,), (0,)), ((), ())), preferred_element_type=jnp.float32
    )


def local(
    residual_in, pre_gain, post_gain, w_gate, w_up, w_down, w_enc, b_enc, threshold, w_dec, b_dec
):
    full_rows = lax.all_gather(residual_in, "mp", axis=1, tiled=True)
    resid_wide = full_rows.astype(jnp.float32)
    normed = (
        resid_wide
        * lax.rsqrt(jnp.mean(resid_wide * resid_wide, axis=1, keepdims=True) + norm_eps)
        * pre_gain[None, :]
    ).astype(jnp.bfloat16)
    gate_out = jnp.dot(normed, w_gate, preferred_element_type=jnp.float32)
    up_out = jnp.dot(normed, w_up, preferred_element_type=jnp.float32)
    hidden = (jax.nn.gelu(gate_out, approximate=True) * up_out).astype(jnp.bfloat16)
    out_share = lax.psum_scatter(
        lax.dot_general(
            w_down, hidden, (((0,), (1,)), ((), ())), preferred_element_type=jnp.float32
        ),
        "mp",
        scatter_dimension=0,
        tiled=True,
    )
    whole_out = lax.all_gather(out_share, "mp", axis=0, tiled=True)
    row_scale = lax.rsqrt(jnp.mean(whole_out * whole_out, axis=0) + norm_eps)
    mixed = resid_wide.T + whole_out * row_scale[None, :] * post_gain[:, None]
    column_rows = mixed.astype(jnp.bfloat16)
    h_cols = lax.all_gather(column_rows, "dp", axis=1, tiled=True)
    pre_act = contract_first(h_cols, w_enc) + b_enc[None, :]
    soft = jax.nn.sigmoid((pre_act - threshold[None, :]) / gate_band)
    feat_bf = (pre_act * soft).astype(jnp.bfloat16)
    gate_part = jnp.sum(soft)
    recon_part = lax.dot_general(
        w_dec, feat_bf, (((0,), (1,)), ((), ())), preferred_element_type=jnp.float32
    )
    recon_all, gate_total = lax.psum((recon_part, gate_part), ("dp", "mp"))
    error_t = recon_all + b_dec[:, None] - h_cols.astype(jnp.float32)
    grad_bdec = jnp.sum(error_t, axis=1)
    square_total = jnp.sum(error_t * error_t)
    err_bf = error_t.astype(jnp.bfloat16)
    loss_value = (0.5 * square_total + sparsity_coef * gate_total) / (
        h_cols.shape[0] * h_cols.shape[1]
    )
    grad_wdec = lax.dot_general(
        feat_bf, err_bf, (((0,), (1,)), ((), ())), preferred_element_type=jnp.float32
    ).astype(jnp.bfloat16)
    grad_feat = lax.dot_general(
        err_bf, w_dec, (((0,), (1,)), ((), ())), preferred_element_type=jnp.float32
    )
    slope = soft * (1.0 - soft) / gate_band
    side_term = (grad_feat * pre_act + sparsity_coef) * slope
    grad_pre = grad_feat * soft + side_term
    grad_thresh = -jnp.sum(side_term, axis=0)
    grad_benc = jnp.sum(grad_pre, axis=0)
    grad_wenc = jnp.dot(
        h_cols, grad_pre.astype(jnp.bfloat16), preferred_element_type=jnp.float32
    ).astype(jnp.bfloat16)
    return (loss_value, grad_wenc, grad_wdec, grad_benc, grad_thresh, grad_bdec)


def solution(mesh):
    placed = (
        P("dp", "mp"),
        P(),
        P(),
        P(None, "mp"),
        P(None, "mp"),
        P("mp", None),
        P(None, ("dp", "mp")),
        P(("dp", "mp")),
        P(("dp", "mp")),
        P(("dp", "mp"), None),
        P(),
    )
    return jax.shard_map(
        local,
        mesh=mesh,
        in_specs=placed,
        out_specs=(
            P(),
            P(None, ("dp", "mp")),
            P(("dp", "mp"), None),
            P(("dp", "mp")),
            P(("dp", "mp")),
            P(),
        ),
        check_vma=False,
    )
```

profile of v0, /device:TPU:0, one launch (start us, length us, event | category | flops | bytes accessed | tf_op | source)
XLA Modules:
  0.0 411.2 jit_solution(16962882458070409448)
XLA Ops:
  7.2 0.0 copy-start
  7.2 0.0 reduce-scatter.4.cloned.1.call-start
  7.2 17.8 %all_gather.9 = bf16[128,3584]{0,1:T(8,128)(2,1)S(1)} all-gather(bf16[128,448]{0,1:T(8,128)(2,1)} %param.11), channel_id=1, replica_groups=mesh['dp'=4,'mp'=8] {'mp'}, dimensions={1}, use_global_device_ids=true | all-gather | bytes 1032192 | tf_op jit(solution)/shard_map/all_gather | solution.py:20
  25.1 0.5 copy.18
  25.6 0.3 fusion.5
  25.9 0.0 copy-done
  25.9 7.5 %fusion.25 = f32[128,1792]{1,0:T(8,128)} fusion(bf16[3584,1792]{1,0:T(8,128)(2,1)} %param.14, bf16[128,3584]{1,0:T(8,128)(2,1)S(1)} %copy.18, f32[3584]{0:T(1024)S(1)} %copy-done, f32[128]{0:T(128)S(1)} %add_rsqrt_fusion.1), kind=kOutput, calls=%fused_computation.40 | convolution fusion | flops 1646002176 | bytes 14694912 | tf_op jit(solution)/shard_map/dot_general | solution.py:27
  33.3 12.8 %convolution_bitcast_fusion.1 = f32[3584,128]{0,1:T(8,128)S(1)} fusion(bf16[1792,3584]{1,0:T(8,128)(2,1)} %param.16, bf16[3584,1792]{1,0:T(8,128)(2,1)} %param.15, f32[128,1792]{1,0:T(8,128)} %fusion.25, bf16[128,3584]{1,0:T(8,128)(2,1)S(1)} %copy.18, f32[3584]{0:T(1024)S(1)} %copy-done, f32[128]{0:T(128)S(1)} %add_rsqrt_fusion.1), kind=kOutput, calls=%fused_computation.5 | convolution fusion | flops 3292463104 | bytes 29374976 | tf_op jit(solution)/shard_map/dot_general | solution.py:31
  46.1 1.7 copy.21
  47.8 0.0 copy-start.1
  47.8 0.0 reduce-scatter.4.cloned.1.call-update
  47.8 0.0 all-gather.3.cloned.1.call-start
  47.9 36.9 %reduce-scatter.4.cloned.1.call-done = f32[448,128]{1,0:T(8,128)} async-done(((f32[3584,128]{1,0:T(8,128)}), f32[448,128]{1,0:T(8,128)}) %reduce-scatter.4.cloned.1.call-update) | async-done | bytes 229392 | tf_op jit(solution)/shard_map/reduce_scatter | solution.py:30
  84.8 0.0 all-gather.3.cloned.1.call-update
  84.8 0.0 all-gather.5.cloned.1.call-start
  84.8 26.5 %all-gather.3.cloned.1.call-done = f32[3584,128]{1,0:T(8,128)} async-done(((f32[448,128]{1,0:T(8,128)}), f32[3584,128]{1,0:T(8,128)}) %all-gather.3.cloned.1.call-update) | async-done | bytes 1835024 | tf_op jit(solution)/shard_map/all_gather | solution.py:38
  111.4 2.0 multiply_reduce_fusion.1
  113.4 0.0 copy-start.5
  113.4 1.8 copy.20
  115.2 0.0 copy-done.1
  115.2 1.3 fusion.4
  116.5 0.0 all-gather.5.cloned.1.call-update
  116.5 0.0 copy-start.6
  116.5 0.2 all-reduce.2.cloned.1.call-start
  116.7 47.5 %all-gather.5.cloned.1.call-done = bf16[3584,512]{0,1:T(8,128)(2,1)} async-done(((bf16[3584,128]{0,1:T(8,128)(2,1)}), bf16[3584,512]{0,1:T(8,128)(2,1)}) %all-gather.5.cloned.1.call-update) | async-done | bytes 3670032 | tf_op jit(solution)/shard_map/all_gather | solution.py:42
  164.3 0.0 copy-done.5
  164.3 0.0 copy-start.3
  164.3 5.3 %convolution_add_fusion = f32[512,512]{1,0:T(8,128)S(1)} fusion(bf16[3584,512]{0,1:T(8,128)(2,1)} %all-gather.5.cloned.1.call-done, bf16[3584,512]{1,0:T(8,128)(2,1)} %param.17, f32[512]{0:T(512)S(1)} %copy-done.5), kind=kOutput, calls=%fused_computation.21 | convolution fusion | flops 1879310336 | bytes 8390656 | tf_op jit(solution)/shard_map/dot_general | solution.py:12
  169.6 0.0 copy-done.6
  169.6 0.0 copy-done.3
  169.6 5.1 %convolution_bitcast_fusion = f32[3584,512]{0,1:T(8,128)} fusion(bf16[512,3584]{1,0:T(8,128)(2,1)S(1)} %copy-done.3, f32[512,512]{1,0:T(8,128)S(1)} %convolution_add_fusion, f32[512]{0:T(512)S(1)} %copy-done.6), kind=kOutput, calls=%fused_computation.2 | convolution fusion | flops 1880883200 | bytes 12060672 | tf_op jit(solution)/shard_map/dot_general | solution.py:47
  174.8 0.0 copy-start.2
  174.8 0.0 all-reduce.2.cloned.1.call-update
  174.8 167.4 %all-reduce.2.cloned.1.call-done = f32[3584,512]{0,1:T(8,128)} async-done(((f32[3584,512]{0,1:T(8,128)}), f32[3584,512]{0,1:T(8,128)}) %all-reduce.2.cloned.1.call-update) | async-done | bytes 7340048 | tf_op jit(solution)/shard_map/psum | solution.py:50
  342.2 0.0 copy-done.2
  342.2 0.0 copy-start.4
  342.2 5.9 %fusion.1 = (f32[3584]{0:T(1024)}, f32[]{:T(128)}, bf16[3584,512]{0,1:T(8,128)(2,1)S(1)}) fusion(bf16[3584,512]{0,1:T(8,128)(2,1)} %all-gather.5.cloned.1.call-done, f32[3584,512]{0,1:T(8,128)} %all-reduce.2.cloned.1.call-done, f32[3584]{0:T(1024)S(1)} %copy-done.2), kind=kLoop, calls=%fused_computation.11 | loop fusion | flops 12841471 | bytes 14708740 | tf_op jit(solution)/shard_map/reduce_sum | solution.py:52
  348.2 0.0 copy-done.4
  348.2 3.1 fusion.32
  351.2 4.0 convolution_convert_fusion
  355.2 40.4 %psum.15 = f32[]{:T(128)} all-reduce(f32[]{:T(128)} %get-tuple-element.13), channel_id=1, replica_groups=mesh['dp'=4,'mp'=8] {'dp','mp'}, use_global_device_ids=true, to_apply=%region_6.0 | all-reduce | flops 1 | bytes 8 | tf_op jit(solution)/shard_map/psum | solution.py:50
  395.7 0.6 neg.7
  397.6 6.0 %convolution_convert_fusion.1 = bf16[3584,512]{1,0:T(8,128)(2,1)} fusion(bf16[3584,512]{0,1:T(8,128)(2,1)} %all-gather.5.cloned.1.call-done, bf16[512,512]{1,0:T(8,128)(2,1)S(1)} %get-tuple-element.11), kind=kOutput, calls=%fused_computation.4 | convolution fusion | flops 1880883200 | bytes 7864320 | tf_op jit(solution)/shard_map/dot_general | solution.py:69
  (2 shorter events, 0.0 us)
Async XLA Ops:
  7.2 18.7 %copy-start = (f32[3584]{0:T(1024)S(1)}, f32[3584]{0:T(1024)}, u32[]{:S(2)}) copy-start(f32[3584]{0:T(1024)} %param.12) | copy-start | bytes 43012
  7.2 77.6 %reduce-scatter.4.cloned.1.call-start = ((), (), s32[]{:S(2)}) async-start(), calls=%async_computation.4 | async-start | bytes 2064384 | tf_op jit(solution)/shard_map/reduce_scatter | solution.py:30
  47.8 67.4 %copy-start.1 = (f32[3584]{0:T(1024)S(1)}, f32[3584]{0:T(1024)}, u32[]{:S(2)}) copy-start(f32[3584]{0:T(1024)} %param.13) | copy-start | bytes 43012
  47.8 63.5 %all-gather.3.cloned.1.call-start = ((), (), s32[]{:S(2)}) async-start(), calls=%async_computation.1 | async-start | bytes 2064384 | tf_op jit(solution)/shard_map/all_gather | solution.py:38
  84.8 79.5 %all-gather.5.cloned.1.call-start = ((), (), s32[]{:S(2)}) async-start(), calls=%async_computation.2 | async-start | bytes 4587520 | tf_op jit(solution)/shard_map/all_gather | solution.py:42
  113.4 50.9 %copy-start.5 = (f32[512]{0:T(512)S(1)}, f32[512]{0:T(512)}, u32[]{:S(2)}) copy-start(f32[512]{0:T(512)} %param.18) | copy-start | bytes 6148
  116.5 53.1 %copy-start.6 = (f32[512]{0:T(512)S(1)}, f32[512]{0:T(512)}, u32[]{:S(2)}) copy-start(f32[512]{0:T(512)} %param.19) | copy-start | bytes 6148
  116.5 225.7 %all-reduce.2.cloned.1.call-start = ((), (), s32[]{:S(2)}) async-start(), calls=%async_computation.3 | async-start | bytes 14680064 | tf_op jit(solution)/shard_map/psum | solution.py:50
  164.3 5.4 %copy-start.3 = (bf16[512,3584]{1,0:T(8,128)(2,1)S(1)}, bf16[512,3584]{1,0:T(8,128)(2,1)}, u32[]{:S(2)}) copy-start(bf16[512,3584]{1,0:T(8,128)(2,1)} %param.20) | copy-start | bytes 11010052
  174.8 167.4 %copy-start.2 = (f32[3584]{0:T(1024)S(1)}, f32[3584]{0:T(1024)}, u32[]{:S(2)}) copy-start(f32[3584]{0:T(1024)} %param.21) | copy-start | bytes 43012
  342.2 5.9 %copy-start.4 = (bf16[512,3584]{1,0:T(8,128)(2,1)S(1)}, bf16[512,3584]{1,0:T(8,128)(2,1)}, u32[]{:S(2)}) copy-start(bf16[512,3584]{1,0:T(8,128)(2,1)} %param.20) | copy-start | bytes 11010052
Sparse Core Ops, SparseCore 0:
  48.0 36.7 reduce-scatter.3
  86.4 24.9 all-gather.2
  116.6 47.6 all-gather.4
  174.9 167.2 all-reduce.1
where the time goes:
time: 412 us; the launch traced here: 411 us
  waiting for transfers between devices  278 us (67%)
  blocking collectives  58.3 us (14%)
  matrix products  43.8 us (11%)
  between operations  16.3 us (4%)
  other arithmetic  10.1 us (2%)
    psum x1, waiting for transfers between devices, local(): recon_all, gate_total = lax.psum((recon_part, gate_part), ('dp', 'mp'))  167 us
    all_gather x1, waiting for transfers between devices, local(): h_cols = lax.all_gather(column_rows, 'dp', axis=1, tiled=True)  47.5 us
    psum x1, blocking collectives, local(): recon_all, gate_total = lax.psum((recon_part, gate_part), ('dp', 'mp'))  40.4 us
    reduce_scatter x1, waiting for transfers between devices, local(): lax.psum_scatter(lax.dot_general(w_down, hidden, (((0,), (1,)), ((), ()))...  36.9 us
    all_gather x1, waiting for transfers between devices, local(): whole_out = lax.all_gather(out_share, 'mp', axis=0, tiled=True)  26.5 us
    all_gather x1, blocking collectives, local(): full_rows = lax.all_gather(residual_in, 'mp', axis=1, tiled=True)  17.8 us
    dot_general x1, matrix products, local(): lax.dot_general(w_down, hidden, (((0,), (1,)), ((), ())), preferred_eleme...  12.8 us
  transfers between devices with their start and end apart: 4, of which 4 were waited for; matrix products, arithmetic and copies ran while one was open for 0% of the time, Pallas kernels for 0%

commit v1 on v0

--- a/solution.py
+++ b/solution.py
@@ -1,3 +1,4 @@
+import functools
 import jax
 import jax.numpy as jnp
 from jax import lax
@@ -6,6 +7,13 @@
 norm_eps = 1e-06
 gate_band = 0.1
 sparsity_coef = 0.05
+
+
+def resolve_boxes(here_x, group_axis, shard_axis):
+    return lax.psum(lax.psum(here_x, axis_name=group_axis), axis_name=shard_axis)
+
+
+use_the_indices = functools.partial(resolve_boxes, group_axis="mp", shard_axis="dp")
 
 
 def contract_first(left, right):
@@ -47,7 +55,7 @@
     recon_part = lax.dot_general(
         w_dec, feat_bf, (((0,), (1,)), ((), ())), preferred_element_type=jnp.float32
     )
-    recon_all, gate_total = lax.psum((recon_part, gate_part), ("dp", "mp"))
+    recon_all, gate_total = use_the_indices((recon_part, gate_part))
     error_t = recon_all + b_dec[:, None] - h_cols.astype(jnp.float32)
     grad_bdec = jnp.sum(error_t, axis=1)
     square_total = jnp.sum(error_t * error_t)

time: 412 us -> 547 us (1.33)
  waiting for transfers between devices: 278 us -> 426 us
  blocking collectives: 58.3 us -> 44.2 us
    psum x1 -> x2, waiting for transfers between devices: 167 us -> 314 us  [the longest x1 159 us: resolve_boxes(): lax.psum(lax.psum(here_x, axis_name=group_axis), axis_name=shard_axis)]
    psum x1 -> x2, blocking collectives: 40.4 us -> 26.3 us  [the longest x1 16.8 us: resolve_boxes(): lax.psum(here_x, axis_name=group_axis)]
  transfers between devices with their start and end apart: 4 -> 5, of which waited for: 4 -> 5; matrix products, arithmetic and copies ran while one was open for 0% -> 0% of each run, Pallas kernels for 0% -> 0%
where the time goes in v1:
time: 547 us; the launch traced here: 546 us
  waiting for transfers between devices  426 us (78%)
  matrix products  45.8 us (8%)
  blocking collectives  44.2 us (8%)
  between operations  16.3 us (3%)
  other arithmetic  10.1 us (2%)
    psum x1, waiting for transfers between devices, resolve_boxes(): lax.psum(lax.psum(here_x, axis_name=group_axis), axis_name=shard_axis)  159 us
    psum x1, waiting for transfers between devices, resolve_boxes(): lax.psum(here_x, axis_name=group_axis)  156 us
    all_gather x1, waiting for transfers between devices, local(): h_cols = lax.all_gather(column_rows, 'dp', axis=1, tiled=True)  47.7 us
    reduce_scatter x1, waiting for transfers between devices, local(): lax.psum_scatter(lax.dot_general(w_down, hidden, (((0,), (1,)), ((), ()))...  37 us
    all_gather x1, waiting for transfers between devices, local(): whole_out = lax.all_gather(out_share, 'mp', axis=0, tiled=True)  26.5 us
    all_gather x1, blocking collectives, local(): full_rows = lax.all_gather(residual_in, 'mp', axis=1, tiled=True)  17.8 us
    psum x1, blocking collectives, resolve_boxes(): lax.psum(here_x, axis_name=group_axis)  16.8 us
    dot_general x1, matrix products, local(): lax.dot_general(w_down, hidden, (((0,), (1,)), ((), ())), preferred_eleme...  12.7 us
  transfers between devices with their start and end apart: 5, of which 5 were waited for; matrix products, arithmetic and copies ran while one was open for 0% of the time, Pallas kernels for 0%

profile of v1, /device:TPU:0, one launch (start us, length us, event | category | flops | bytes accessed | tf_op | source)
XLA Modules:
  0.0 546.4 jit_solution(10705825602551404186)
XLA Ops:
  7.2 0.0 copy-start.1
  7.2 0.0 reduce-scatter.4.cloned.1.call-start
  7.2 17.8 %all_gather.9 = bf16[128,3584]{0,1:T(8,128)(2,1)S(1)} all-gather(bf16[128,448]{0,1:T(8,128)(2,1)} %param.11), channel_id=1, replica_groups=mesh['dp'=4,'mp'=8] {'mp'}, dimensions={1}, use_global_device_ids=true | all-gather | bytes 1032192 | tf_op jit(solution)/shard_map/all_gather | solution.py:28
  25.1 0.5 copy.18
  25.6 0.3 fusion.5
  25.9 0.0 copy-done.1
  25.9 7.5 %fusion.25 = f32[128,1792]{1,0:T(8,128)} fusion(bf16[3584,1792]{1,0:T(8,128)(2,1)} %param.14, bf16[128,3584]{1,0:T(8,128)(2,1)S(1)} %copy.18, f32[3584]{0:T(1024)S(1)} %copy-done.1, f32[128]{0:T(128)S(1)} %add_rsqrt_fusion.1), kind=kOutput, calls=%fused_computation.40 | convolution fusion | flops 1646002176 | bytes 14694912 | tf_op jit(solution)/shard_map/dot_general | solution.py:35
  33.3 12.7 %convolution_bitcast_fusion.1 = f32[3584,128]{0,1:T(8,128)S(1)} fusion(bf16[1792,3584]{1,0:T(8,128)(2,1)} %param.16, bf16[3584,1792]{1,0:T(8,128)(2,1)} %param.15, f32[128,1792]{1,0:T(8,128)} %fusion.25, bf16[128,3584]{1,0:T(8,128)(2,1)S(1)} %copy.18, f32[3584]{0:T(1024)S(1)} %copy-done.1, f32[128]{0:T(128)S(1)} %add_rsqrt_fusion.1), kind=kOutput, calls=%fused_computation.5 | convolution fusion | flops 3292463104 | bytes 29374976 | tf_op jit(solution)/shard_map/dot_general | solution.py:39
  46.1 1.7 copy.21
  47.7 0.0 copy-start.2
  47.7 0.0 reduce-scatter.4.cloned.1.call-update
  47.8 0.0 all-gather.3.cloned.1.call-start
  47.8 37.0 %reduce-scatter.4.cloned.1.call-done = f32[448,128]{1,0:T(8,128)} async-done(((f32[3584,128]{1,0:T(8,128)}), f32[448,128]{1,0:T(8,128)}) %reduce-scatter.4.cloned.1.call-update) | async-done | bytes 229392 | tf_op jit(solution)/shard_map/reduce_scatter | solution.py:38
  84.8 0.0 all-gather.3.cloned.1.call-update
  84.8 0.0 all-gather.5.cloned.1.call-start
  84.9 26.5 %all-gather.3.cloned.1.call-done = f32[3584,128]{1,0:T(8,128)} async-done(((f32[448,128]{1,0:T(8,128)}), f32[3584,128]{1,0:T(8,128)}) %all-gather.3.cloned.1.call-update) | async-done | bytes 1835024 | tf_op jit(solution)/shard_map/all_gather | solution.py:46
  111.4 2.0 multiply_reduce_fusion.1
  113.4 0.0 copy-start.6
  113.4 1.8 copy.20
  115.3 0.0 copy-done.2
  115.3 1.3 fusion.4
  116.5 0.0 all-gather.5.cloned.1.call-update
  116.6 0.0 copy-start.7
  116.6 0.0 all-reduce.3.cloned.1.call-start
  116.6 47.7 %all-gather.5.cloned.1.call-done = bf16[3584,512]{0,1:T(8,128)(2,1)} async-done(((bf16[3584,128]{0,1:T(8,128)(2,1)}), bf16[3584,512]{0,1:T(8,128)(2,1)}) %all-gather.5.cloned.1.call-update) | async-done | bytes 3670032 | tf_op jit(solution)/shard_map/all_gather | solution.py:50
  164.3 0.0 copy-done.6
  164.3 0.0 copy-start.4
  164.3 5.3 convolution_add_fusion
  169.7 0.0 copy-done.7
  169.7 0.0 copy-done.4
  169.7 5.2 convolution_bitcast_fusion
  174.9 0.0 all-reduce.3.cloned.1.call-update
  174.9 0.2 all-reduce.5.cloned.1.call-start
  175.1 155.7 %all-reduce.3.cloned.1.call-done = f32[3584,512]{0,1:T(8,128)} async-done(((f32[3584,512]{0,1:T(8,128)}), f32[3584,512]{0,1:T(8,128)}) %all-reduce.3.cloned.1.call-update) | async-done | bytes 7340048 | tf_op jit(solution)/shard_map/psum | solution.py:13
  330.8 0.0 copy-start.3
  330.8 0.0 all-reduce.5.cloned.1.call-update
  330.8 158.7 %all-reduce.5.cloned.1.call-done = f32[3584,512]{0,1:T(8,128)} async-done(((f32[3584,512]{0,1:T(8,128)}), f32[3584,512]{0,1:T(8,128)}) %all-reduce.5.cloned.1.call-update) | async-done | bytes 7340048 | tf_op jit(solution)/shard_map/psum | solution.py:13
  489.5 0.0 copy-done.3
  489.5 0.0 copy-start.5
  489.5 5.9 %fusion.1 = (f32[3584]{0:T(1024)}, f32[]{:T(128)}, bf16[3584,512]{0,1:T(8,128)(2,1)S(1)}) fusion(bf16[3584,512]{0,1:T(8,128)(2,1)} %all-gather.5.cloned.1.call-done, f32[3584,512]{0,1:T(8,128)} %all-reduce.5.cloned.1.call-done, f32[3584]{0:T(1024)S(1)} %copy-done.3), kind=kLoop, calls=%fused_computation.11 | loop fusion | flops 12841471 | bytes 14708740 | tf_op jit(solution)/shard_map/reduce_sum | solution.py:60
  495.4 0.0 copy-done.5
  495.4 3.1 fusion.32
  498.5 0.0 copy-done
  498.5 16.8 %psum.30 = f32[]{:T(128)} all-reduce(f32[]{:T(128)} %get-tuple-element.13), channel_id=1, replica_groups=mesh['dp'=4,'mp'=8] {'mp'}, use_global_device_ids=true, to_apply=%region_7.0 | all-reduce | flops 1 | bytes 8 | tf_op jit(solution)/shard_map/psum | solution.py:13
  515.3 6.0 %convolution_convert_fusion = bf16[512,3584]{1,0:T(8,128)(2,1)} fusion(bf16[3584,512]{0,1:T(8,128)(2,1)} %copy-done, f32[512,512]{1,0:T(8,128)S(1)} %convolution_add_fusion, f32[512]{0:T(512)S(1)} %copy-done.7), kind=kOutput, calls=%fused_computation.3 | convolution fusion | flops 1882718208 | bytes 8390656 | tf_op jit(solution)/shard_map/dot_general | solution.py:66
  521.4 9.5 %psum.31 = f32[]{:T(128)} all-reduce(f32[]{:T(128)} %psum.30), channel_id=1, replica_groups=mesh['dp'=4,'mp'=8] {'dp'}, use_global_device_ids=true, to_apply=%region_8.0 | all-reduce | flops 1 | bytes 8 | tf_op jit(solution)/shard_map/psum | solution.py:13
  530.9 0.6 neg.7
  532.8 6.0 %convolution_convert_fusion.1 = bf16[3584,512]{1,0:T(8,128)(2,1)} fusion(bf16[3584,512]{0,1:T(8,128)(2,1)} %all-gather.5.cloned.1.call-done, bf16[512,512]{1,0:T(8,128)(2,1)S(1)} %get-tuple-element.11), kind=kOutput, calls=%fused_computation.4 | convolution fusion | flops 1880883200 | bytes 7864320 | tf_op jit(solution)/shard_map/dot_general | solution.py:77
  (3 shorter events, 0.0 us)
Async XLA Ops:
  7.2 18.7 %copy-start.1 = (f32[3584]{0:T(1024)S(1)}, f32[3584]{0:T(1024)}, u32[]{:S(2)}) copy-start(f32[3584]{0:T(1024)} %param.12) | copy-start | bytes 43012
  7.2 77.6 %reduce-scatter.4.cloned.1.call-start = ((), (), s32[]{:S(2)}) async-start(), calls=%async_computation.5 | async-start | bytes 2064384 | tf_op jit(solution)/shard_map/reduce_scatter | solution.py:38
  47.7 67.5 %copy-start.2 = (f32[3584]{0:T(1024)S(1)}, f32[3584]{0:T(1024)}, u32[]{:S(2)}) copy-start(f32[3584]{0:T(1024)} %param.13) | copy-start | bytes 43012
  47.8 63.7 %all-gather.3.cloned.1.call-start = ((), (), s32[]{:S(2)}) async-start(), calls=%async_computation.1 | async-start | bytes 2064384 | tf_op jit(solution)/shard_map/all_gather | solution.py:46
  84.8 79.5 %all-gather.5.cloned.1.call-start = ((), (), s32[]{:S(2)}) async-start(), calls=%async_computation.2 | async-start | bytes 4587520 | tf_op jit(solution)/shard_map/all_gather | solution.py:50
  113.4 50.9 %copy-start.6 = (f32[512]{0:T(512)S(1)}, f32[512]{0:T(512)}, u32[]{:S(2)}) copy-start(f32[512]{0:T(512)} %param.18) | copy-start | bytes 6148
  116.6 53.1 %copy-start.7 = (f32[512]{0:T(512)S(1)}, f32[512]{0:T(512)}, u32[]{:S(2)}) copy-start(f32[512]{0:T(512)} %param.19) | copy-start | bytes 6148
  116.6 214.2 %all-reduce.3.cloned.1.call-start = ((), (), s32[]{:S(2)}) async-start(), calls=%async_computation.3 | async-start | bytes 14680064 | tf_op jit(solution)/shard_map/psum | solution.py:13
  164.3 5.4 copy-start.4
  174.9 314.6 %all-reduce.5.cloned.1.call-start = ((), (), s32[]{:S(2)}) async-start(), calls=%async_computation.4 | async-start | bytes 14680064 | tf_op jit(solution)/shard_map/psum | solution.py:13
  330.8 158.7 %copy-start.3 = (f32[3584]{0:T(1024)S(1)}, f32[3584]{0:T(1024)}, u32[]{:S(2)}) copy-start(f32[3584]{0:T(1024)} %param.21) | copy-start | bytes 43012
  489.5 6.0 %copy-start.5 = (bf16[512,3584]{1,0:T(8,128)(2,1)S(1)}, bf16[512,3584]{1,0:T(8,128)(2,1)}, u32[]{:S(2)}) copy-start(bf16[512,3584]{1,0:T(8,128)(2,1)} %param.20) | copy-start | bytes 11010052
  495.4 3.1 copy-start
Sparse Core Ops, SparseCore 0:
  47.9 36.8 reduce-scatter.3
  86.5 24.9 all-gather.2
  116.7 47.6 all-gather.4
  175.0 155.7 all-reduce.2
  334.0 155.4 all-reduce.4
